TPU v7x, 128 devices: a whole 4x4x4 slice. The times are simulated.
128 devices in a mesh: dom: 16 (over x, y), cls: 8 (over z, core).
Axes of the slice: x: 4, y: 4, z: 4, core: 2. Of those that a mesh axis runs over, the one named last changes fastest.
Arguments:
- stack: bfloat16 [32768, 2, 64, 128], P(('dom', 'cls')), may hold values from -6 to 6
- batch_index: int32 [16384], P(('dom', 'cls')), may hold values from 0 to 255, as said below
- best_class: int32 [16384], P(('dom', 'cls')), may hold values from 0 to 511, as said below
- best_rot: int32 [16384], P(('dom', 'cls')), may hold values from 0 to 63
- best_shift: int32 [16384, 2], P(('dom', 'cls')), may hold values from -4 to 4
- ctf: bfloat16 [16384, 64], P(('dom', 'cls')), may hold values from -1 to 1
- averages: float32 [512, 2, 64, 128], P(('dom', 'cls')), may hold values from -6 to 6
- velocity: float32 [512, 2, 64, 128], P(('dom', 'cls')), may hold values from -3 to 3
Outputs:
- new_averages: float32 [512, 2, 64, 128], P(('dom', 'cls'))
- new_velocity: float32 [512, 2, 64, 128], P(('dom', 'cls'))
- errors: float32 [16384], P(('dom', 'cls'))
Inputs may be any that keep to these rules, and one draw needn't show every extreme that they name: `batch_index`: each aligned block of 128 entries (one device's particles) holds distinct row numbers into that device's own 256 rows of stack. `best_class`: classes c with equal c // 32 form a group. In each aligned block of 128 entries (one device's particles) at most 16 entries name classes of one group, and some group is named by exactly 16 entries of that block.
All inputs are finite; a program needn't handle non-finite values.
Results may differ from a plain program's by a relative error of at most 0.0026.
Values may be sent and summed in bfloat16 or wider, within the bound.
No kernel may reach another device: no remote copies, remote signals or barrier semaphores. Data moves between devices by JAX's collectives and lax.ppermute only.
A program may use at most 128 MiB of HBM per device.

v0:
```python
import jax
import jax.numpy as jnp
from jax import lax
from jax.sharding import PartitionSpec as P

IMG = 128
TWO_PI = 6.283185307179586
MOMENTUM = 0.9
RATE = 0.5
RIDGE = 1.0


def align_rows(rows, rotation, shift):
    cycles = rows.shape[2]
    angles = rows.shape[3]
    radius = jnp.arange(cycles).astype(jnp.float32) + 1.0
    theta = TWO_PI * jnp.arange(angles).astype(jnp.float32) / angles
    shift_x = shift[:, 0].astype(jnp.float32)
    shift_y = shift[:, 1].astype(jnp.float32)
    along = (
        jnp.cos(theta)[None, None, :] * shift_x[:, None, None]
        + jnp.sin(theta)[None, None, :] * shift_y[:, None, None]
    )
    phase = TWO_PI * radius[None, :, None] * along / IMG
    cosine = jnp.cos(phase)
    sine = jnp.sin(phase)
    real = rows[:, 0].astype(jnp.float32)
    imag = rows[:, 1].astype(jnp.float32)
    turned = jnp.stack([cosine * real - sine * imag, sine * real + cosine * imag], axis=1).astype(
        jnp.bfloat16
    )
    source = (jnp.arange(angles)[None, :] + 2 * rotation[:, None]) % angles
    permute = (source[:, :, None] == jnp.arange(angles)[None, None, :]).astype(jnp.bfloat16)
    moved = jnp.einsum("pskb,pab->pska", turned, permute, preferred_element_type=jnp.float32)
    return moved.astype(jnp.bfloat16)


def class_table(marker, column):
    local = marker.astype(jnp.int32) - 1
    return (jnp.arange(column)[:, None] == local[None, :]).astype(jnp.bfloat16)


def class_partials(table, terms, gamma):
    grads = jnp.dot(table, terms, preferred_element_type=jnp.float32)
    gamma_float = gamma.astype(jnp.float32)
    weights = jnp.dot(
        table.astype(jnp.float32),
        gamma_float * gamma_float,
        precision=lax.Precision.HIGHEST,
        preferred_element_type=jnp.float32,
    )
    return (grads, weights)


def on_device(stack, batch_index, best_class, best_rot, best_shift, ctf, averages, velocity):
    count = batch_index.shape[0]
    cycles = ctf.shape[1]
    angles = stack.shape[3]
    stored = stack.shape[0]
    flat = 2 * cycles * angles
    owners = lax.axis_size("dom")
    column = lax.axis_size("cls") * averages.shape[0]
    slots = 2 * count // owners
    buffer_rows = owners * slots
    picker = (batch_index[:, None] == jnp.arange(stored)[None, :]).astype(jnp.bfloat16)
    rows = jnp.dot(picker, stack.reshape(stored, flat), preferred_element_type=jnp.float32)
    rows = rows.astype(jnp.bfloat16).reshape(count, 2, cycles, angles)
    aligned = align_rows(rows, best_rot, best_shift)
    owner = best_class // column
    local_class = best_class - owner * column
    placed = (owner[:, None] == jnp.arange(owners)[None, :]).astype(jnp.int32)
    position = jnp.sum(jnp.cumsum(placed, axis=0) * placed, axis=1) - 1
    target = owner * slots + position
    dispatch = (jnp.arange(buffer_rows)[:, None] == target[None, :]).astype(jnp.bfloat16)

    def pack(payload):
        packed = jnp.dot(dispatch, payload, preferred_element_type=jnp.float32).astype(jnp.bfloat16)
        return packed.reshape(owners, slots, payload.shape[1])

    ctf_packed = pack(ctf)
    marker_packed = pack((local_class + 1).astype(jnp.bfloat16)[:, None]).reshape(owners, slots)
    every = lax.all_gather(averages.astype(jnp.bfloat16), ("dom", "cls"), axis=0, tiled=True)
    total_classes = every.shape[0]
    chooser = (best_class[:, None] == jnp.arange(total_classes)[None, :]).astype(jnp.bfloat16)
    model = jnp.dot(
        chooser, every.reshape(total_classes, flat), preferred_element_type=jnp.float32
    ).reshape(count, 2, cycles, angles)
    gamma_wide = ctf.astype(jnp.float32)[:, None, :, None]
    resid = aligned.astype(jnp.float32) - gamma_wide * model
    errors = jnp.mean(resid * resid, axis=(1, 2, 3))
    term = (gamma_wide * resid).astype(jnp.bfloat16).reshape(count, flat)
    arrived = (
        lax.all_to_all(pack(term), "dom", split_axis=0, concat_axis=0, tiled=True),
        lax.all_to_all(ctf_packed, "dom", split_axis=0, concat_axis=0, tiled=True),
        lax.all_to_all(marker_packed, "dom", split_axis=0, concat_axis=0, tiled=True),
    )
    got_terms = arrived[0].reshape(buffer_rows, flat)
    got_gamma = arrived[1].reshape(buffer_rows, cycles)
    table = class_table(arrived[2].reshape(buffer_rows), column)
    grads, weights = class_partials(table, got_terms, got_gamma)
    summed, weight_sum = (
        lax.psum_scatter(grads, "cls", scatter_dimension=0, tiled=True),
        lax.psum_scatter(weights, "cls", scatter_dimension=0, tiled=True),
    )
    step = (summed.reshape(averages.shape) - RIDGE * averages) / (
        weight_sum[:, None, :, None] + RIDGE
    )
    new_velocity = MOMENTUM * velocity + step
    new_averages = averages + RATE * new_velocity
    return (new_averages, new_velocity, errors)


def solution(mesh):
    in_specs = (
        P(("dom", "cls"), None, None, None),
        P(("dom", "cls")),
        P(("dom", "cls")),
        P(("dom", "cls")),
        P(("dom", "cls"), None),
        P(("dom", "cls"), None),
        P(("dom", "cls"), None, None, None),
        P(("dom", "cls"), None, None, None),
    )
    out_specs = (
        P(("dom", "cls"), None, None, None),
        P(("dom", "cls"), None, None, None),
        P(("dom", "cls")),
    )
    return jax.shard_map(
        on_device, mesh=mesh, in_specs=in_specs, out_specs=out_specs, check_vma=False
    )
```

profile of v0, /device:TPU:0, one launch (start us, length us, event | category | flops | bytes accessed | tf_op | source)
XLA Modules:
  0.0 396.0 jit_solution(6878493428379385242)
XLA Ops:
  7.2 0.0 all-gather.2.cloned.1.call-start
  7.2 1.6 convert_element_type.118
  8.8 0.0 all-gather.2.cloned.1.call-update
  8.9 0.7 and_select_fusion
  9.5 0.1 fusion.38
  9.6 0.2 reduce_window_sum.11
  9.8 0.2 select_reduce_fusion
  10.0 0.7 add_add_fusion
  10.6 0.8 fusion.30
  11.4 0.7 all_to_all.16
  12.2 7.1 %all-to-all-start = ((bf16[16,1,16]{2,1,0:T(2,128)(2,1)}), bf16[16,1,16]{2,1,0:T(2,128)(2,1)S(1)}, u32[]{:S(2)}, u32[]{:S(2)}) async-start(bf16[16,1,16]{2,1,0:T(2,128)(2,1)} %all_to_all.16), calls=%async_computation | async-start | bytes 16384 | tf_op jit(solution)/shard_map/all_to_all | solution.py:95
  19.3 0.8 copy.19
  20.1 8.8 %fusion.24 = bf16[16,8,128,128]{3,1,2,0:T(8,128)(2,1)S(1)} fusion(bf16[32,8,128,128]{3,2,1,0:T(8,128)(2,1)} %bitcast.59, s32[128]{0:T(128)} %param.9), kind=kOutput, calls=%fused_computation.30 | convolution fusion | flops 1075871744 | bytes 12583424 | tf_op jit(solution)/shard_map/dot_general | solution.py:66
  28.9 0.0 copy-start.5
  28.9 0.0 copy-start.3
  28.9 1.2 copy.27
  30.3 0.0 copy-done.5
  30.3 0.0 copy-done.3
  30.3 0.1 add_select_fusion
  30.4 0.1 multiply_add_fusion.1
  30.5 17.4 %fusion.8 = (bf16[128,1,64,128]{3,2,1,0:T(8,128)(2,1)S(1)}, bf16[128,1,64,128]{3,2,1,0:T(8,128)(2,1)}) fusion(f32[128,128]{1,0:T(8,128)S(1)} %multiply_add_fusion.1, f32[64]{0:T(128)S(1)} %add_multiply_fusion, bf16[128,2,64,128]{3,2,1,0:T(8,128)(2,1)S(1)} %bitcast.58), kind=kLoop, calls=%fused_computation.17 | loop fusion | flops 12582912 | bytes 8454400 | tf_op jit(solution)/shard_map/convert
  47.9 0.0 copy-start.4
  47.9 46.7 %all-gather.2.cloned.1.call-done = bf16[512,2,64,128]{3,2,1,0:T(8,128)(2,1)} async-done(((bf16[4,2,64,128]{3,2,1,0:T(8,128)(2,1)}), bf16[512,2,64,128]{3,2,1,0:T(8,128)(2,1)}) %all-gather.2.cloned.1.call-update) | async-done | bytes 16777232 | tf_op jit(solution)/shard_map/all_gather | solution.py:82
  94.6 23.9 %copy.25 = bf16[512,2,64,128]{0,3,2,1:T(8,128)(2,1)} copy(bf16[512,2,64,128]{3,2,1,0:T(8,128)(2,1)} %all-gather.2.cloned.1.call-done) | data formatting | bytes 33554432 | tf_op jit(solution)/shard_map/reshape | solution.py:86
  118.5 0.0 copy-done.4
  118.5 13.6 %fusion = f32[128,2,64,128]{0,3,2,1:T(8,128)} fusion(bf16[512,2,64,128]{0,3,2,1:T(8,128)(2,1)} %copy.25, s32[128]{0:T(128)S(1)} %copy-done.4), kind=kOutput, calls=%fused_computation.2 | convolution fusion | flops 2147549184 | bytes 25166336 | tf_op jit(solution)/shard_map/dot_general | solution.py:85
  132.1 8.7 %copy.21 = f32[128,2,64,128]{3,2,1,0:T(8,128)} copy(f32[128,2,64,128]{0,3,2,1:T(8,128)} %fusion) | data formatting | bytes 16777216 | tf_op jit(solution)/shard_map/dot_general | solution.py:85
  140.8 9.4 %multiply_reduce_fusion = (f32[128]{0:T(128)S(1)}, bf16[128,2,64,128]{3,2,1,0:T(8,128)(2,1)S(1)}) fusion(f32[128,2,64,128]{3,2,1,0:T(8,128)} %copy.21, f32[128,64]{1,0:T(8,128)S(1)} %copy.19, s32[128,128]{1,0:T(8,128)S(1)} %add_select_fusion, bf16[128,1,64,128]{3,2,1,0:T(8,128)(2,1)} %get-tuple-element.8, bf16[128,1,64,128]{3,2,1,0:T(8,128)(2,1)S(1)} %get-tuple-element.7), kind=kOutput, calls=%fused_computation.6 | convolution fusion | flops 557842304 | bytes 16876032 | tf_op jit(solution)/shard_map/pskb,pab->pska/dot_general | solution.py:34
  150.2 6.7 %convolution_convert_fusion = bf16[256,16384]{1,0:T(8,128)(2,1)} fusion(bf16[16,8,128,128]{3,2,1,0:T(8,128)(2,1)S(1)} %bitcast.60, s32[128]{0:T(128)S(1)} %add_add_fusion), kind=kOutput, calls=%fused_computation | convolution fusion | flops 1077968896 | bytes 12583424 | tf_op jit(solution)/shard_map/dot_general | solution.py:77
  156.9 0.0 all-to-all-done
  156.9 6.9 %all-to-all-start.1 = ((bf16[16,16,16384]{2,1,0:T(8,128)(2,1)}), bf16[16,16,16384]{2,1,0:T(8,128)(2,1)}, u32[]{:S(2)}, u32[]{:S(2)}) async-start(bf16[16,16,16384]{2,1,0:T(8,128)(2,1)} %bitcast.57), calls=%async_computation.1 | async-start | bytes 16777216 | tf_op jit(solution)/shard_map/all_to_all | solution.py:93
  163.8 0.0 all-reduce.4.cloned.1.call-start
  163.9 0.1 sub.32
  163.9 146.1 %all-to-all-done.1 = bf16[16,16,16384]{2,1,0:T(8,128)(2,1)} async-done(((bf16[16,16,16384]{2,1,0:T(8,128)(2,1)}), bf16[16,16,16384]{2,1,0:T(8,128)(2,1)}, u32[]{:S(2)}, u32[]{:S(2)}) %all-to-all-start.1) | async-done | bytes 8388640 | tf_op jit(solution)/shard_map/all_to_all | solution.py:93
  310.0 0.0 copy-start.2
  310.0 0.0 copy-start.6
  310.0 0.0 copy-start
  310.0 0.0 copy-start.1
  310.0 6.3 %fusion.41 = f32[32,16384]{1,0:T(8,128)} fusion(bf16[256,16384]{1,0:T(8,128)(2,1)} %bitcast.12, s32[256]{0:T(256)S(1)} %sub.32), kind=kOutput, calls=%fused_computation.59 | convolution fusion | flops 268443648 | bytes 10486784 | tf_op jit(solution)/shard_map/dot_general | solution.py:44
  316.3 0.0 all-reduce.4.cloned.1.call-update
  316.4 0.0 copy-done.2
  316.4 0.1 convolution_convert_fusion.2
  316.5 0.1 copy.22
  316.7 0.7 reshape.217
  317.4 11.7 %all-to-all-start.2 = ((bf16[16,2,512]{2,1,0:T(2,128)(2,1)}), bf16[16,2,512]{2,1,0:T(2,128)(2,1)S(1)}, u32[]{:S(2)}, u32[]{:S(2)}) async-start(bf16[16,2,512]{2,1,0:T(2,128)(2,1)} %reshape.217), calls=%async_computation.2 | async-start | bytes 65536 | tf_op jit(solution)/shard_map/all_to_all | solution.py:94
  329.1 0.0 copy-done.6
  329.1 0.6 dynamic-slice
  330.3 6.4 %all-to-all-done.2 = bf16[16,2,512]{2,1,0:T(2,128)(2,1)S(1)} async-done(((bf16[16,2,512]{2,1,0:T(2,128)(2,1)}), bf16[16,2,512]{2,1,0:T(2,128)(2,1)S(1)}, u32[]{:S(2)}, u32[]{:S(2)}) %all-to-all-start.2) | async-done | bytes 32800 | tf_op jit(solution)/shard_map/all_to_all | solution.py:94
  336.7 0.1 reshape.218
  336.8 0.2 fusion.40
  337.0 23.6 %all-reduce.1 = f32[32,64]{1,0:T(8,128)S(1)} all-reduce(f32[32,64]{1,0:T(8,128)S(1)} %fusion.40), channel_id=3, replica_groups=mesh['dom'=16,'cls'=8] {'cls'}, use_global_device_ids=true, to_apply=%region_3.4.clone | all-reduce | flops 2048 | bytes 16384
  360.6 0.5 broadcast_multiply_fusion
  361.1 26.0 %all-reduce.4.cloned.1.call-done = f32[32,16384]{1,0:T(8,128)} async-done(((f32[32,16384]{1,0:T(8,128)}), f32[32,16384]{1,0:T(8,128)}) %all-reduce.4.cloned.1.call-update) | async-done | bytes 2097168
  387.0 1.1 dynamic-slice_bitcast_fusion
  388.2 0.0 copy-done
  388.2 0.0 copy-done.1
  388.2 1.0 multiply_add_fusion
  (9 shorter events, 0.1 us)
Async XLA Ops:
  7.2 87.4 %all-gather.2.cloned.1.call-start = ((), (), s32[]{:S(2)}) async-start(), calls=%async_computation.3 | async-start | bytes 16908288 | tf_op jit(solution)/shard_map/all_gather | solution.py:82
  12.2 144.8 %all-to-all-start = ((bf16[16,1,16]{2,1,0:T(2,128)(2,1)}), bf16[16,1,16]{2,1,0:T(2,128)(2,1)S(1)}, u32[]{:S(2)}, u32[]{:S(2)}) async-start(bf16[16,1,16]{2,1,0:T(2,128)(2,1)} %all_to_all.16), calls=%async_computation | async-start | bytes 16384 | tf_op jit(solution)/shard_map/all_to_all | solution.py:95
  28.9 1.3 copy-start.5
  28.9 1.3 copy-start.3
  47.9 70.6 %copy-start.4 = (s32[128]{0:T(128)S(1)}, s32[128]{0:T(128)}, u32[]{:S(2)}) copy-start(s32[128]{0:T(128)} %param.10) | copy-start | bytes 1540
  156.9 153.1 %all-to-all-start.1 = ((bf16[16,16,16384]{2,1,0:T(8,128)(2,1)}), bf16[16,16,16384]{2,1,0:T(8,128)(2,1)}, u32[]{:S(2)}, u32[]{:S(2)}) async-start(bf16[16,16,16384]{2,1,0:T(8,128)(2,1)} %bitcast.57), calls=%async_computation.1 | async-start | bytes 16777216 | tf_op jit(solution)/shard_map/all_to_all | solution.py:93
  163.8 223.3 %all-reduce.4.cloned.1.call-start = ((), (), s32[]{:S(2)}) async-start(), calls=%async_computation.4 | async-start | bytes 4194304
  310.0 6.3 %copy-start.2 = (bf16[128,64]{0,1:T(8,128)(2,1)S(1)}, bf16[128,64]{0,1:T(8,128)(2,1)}, u32[]{:S(2)}) copy-start(bf16[128,64]{0,1:T(8,128)(2,1)} %param.13) | copy-start | bytes 49156
  310.0 19.1 %copy-start.6 = (u32[128]{0:T(128)S(1)}, u32[128]{0:T(128)}, u32[]{:S(2)}) copy-start(u32[128]{0:T(128)} %constant.71) | copy-start | bytes 1540
  310.0 78.1 %copy-start = (f32[4,2,64,128]{3,2,1,0:T(8,128)S(1)}, f32[4,2,64,128]{3,2,1,0:T(8,128)}, u32[]{:S(2)}) copy-start(f32[4,2,64,128]{3,2,1,0:T(8,128)} %param.14) | copy-start | bytes 786436
  310.0 78.1 %copy-start.1 = (f32[4,2,64,128]{3,2,1,0:T(8,128)S(1)}, f32[4,2,64,128]{3,2,1,0:T(8,128)}, u32[]{:S(2)}) copy-start(f32[4,2,64,128]{3,2,1,0:T(8,128)} %param.15) | copy-start | bytes 786436
  317.4 19.3 %all-to-all-start.2 = ((bf16[16,2,512]{2,1,0:T(2,128)(2,1)}), bf16[16,2,512]{2,1,0:T(2,128)(2,1)S(1)}, u32[]{:S(2)}, u32[]{:S(2)}) async-start(bf16[16,2,512]{2,1,0:T(2,128)(2,1)} %reshape.217), calls=%async_computation.2 | async-start | bytes 65536 | tf_op jit(solution)/shard_map/all_to_all | solution.py:94
Sparse Core Ops, SparseCore 0:
  11.7 82.8 all-gather.1
  316.5 70.5 all-reduce.3
where the time goes:
time: 397 us; the launch traced here: 396 us
  waiting for transfers between devices  225 us (57%)
  matrix products  45.9 us (12%)
  local copies, waits for them, and re-layouts  38.1 us (10%)
  starting transfers between devices  25.8 us (6%)
  blocking collectives  23.6 us (6%)
  other arithmetic  22.6 us (6%)
  between operations  14.9 us (4%)
    all_to_all x1, waiting for transfers between devices, on_device(): lax.all_to_all(pack(term), 'dom', split_axis=0, concat_axis=0, tiled=True)  146 us
    all_gather x1, waiting for transfers between devices, on_device(): lax.all_gather(averages.astype(jnp.bfloat16), ('dom', 'cls'), axis=0, til...  46.7 us
    unnamed x3, waiting for transfers between devices  26 us
    reshape x1, local copies, waits for them, and re-layouts, on_device(): every.reshape(total_classes, flat)  23.9 us
    unnamed x1, blocking collectives  23.6 us
    another operation x1, other arithmetic  17.4 us
    dot_general x1, matrix products, on_device(): jnp.dot(chooser, every.reshape(total_classes, flat), preferred_element_ty...  13.6 us
    all_to_all x1, starting transfers between devices, on_device(): lax.all_to_all(ctf_packed, 'dom', split_axis=0, concat_axis=0, tiled=True)  11.7 us
  transfers between devices with their start and end apart: 5, of which 4 were waited for; matrix products, arithmetic and copies ran while one was open for 24% of the time, Pallas kernels for 0%

commit v1 on v0

--- a/solution.py
+++ b/solution.py
@@ -8,6 +8,22 @@
 MOMENTUM = 0.9
 RATE = 0.5
 RIDGE = 1.0
+
+
+def pairwise_exchange(array, axis, split, join):
+    ways, here = (lax.axis_size(axis), lax.axis_index(axis))
+    width = array.shape[split] // ways
+    lengths = list(array.shape)
+    lengths[split] = width
+    height = lengths[join]
+    lengths[join] = height * ways
+    full = jnp.zeros(lengths, array.dtype)
+    for mask in range(ways):
+        part = lax.dynamic_slice_in_dim(array, (here ^ mask) * width, width, axis=split)
+        if mask:
+            part = lax.ppermute(part, axis, [(d, d ^ mask) for d in range(ways)])
+        full = lax.dynamic_update_slice_in_dim(full, part, (here ^ mask) * height, axis=join)
+    return full
 
 
 def align_rows(rows, rotation, shift):
@@ -90,7 +106,7 @@
     errors = jnp.mean(resid * resid, axis=(1, 2, 3))
     term = (gamma_wide * resid).astype(jnp.bfloat16).reshape(count, flat)
     arrived = (
-        lax.all_to_all(pack(term), "dom", split_axis=0, concat_axis=0, tiled=True),
+        pairwise_exchange(pack(term), "dom", 0, 0),
         lax.all_to_all(ctf_packed, "dom", split_axis=0, concat_axis=0, tiled=True),
         lax.all_to_all(marker_packed, "dom", split_axis=0, concat_axis=0, tiled=True),
     )

time: 397 us -> 400 us (level)
  waiting for transfers between devices: 225 us -> 188 us
  local copies, waits for them, and re-layouts: 38.1 us -> 58.8 us
  blocking collectives: 23.6 us -> 38.4 us
  starting transfers between devices: 25.8 us -> 33.4 us
    all_to_all x2 -> x0, waiting for transfers between devices: 146 us -> none  [the longest x1 146 us: on_device(): lax.all_to_all(pack(term), 'dom', split_axis=0, concat_axis=0, tiled=True)]
    ppermute x0 -> x15, waiting for transfers between devices: none -> 102 us  [pairwise_exchange(): part = lax.ppermute(part, axis, [(d, d ^ mask) for d in range(ways)])]
    ppermute x0 -> x15, starting transfers between devices: none -> 29.3 us  [pairwise_exchange(): part = lax.ppermute(part, axis, [(d, d ^ mask) for d in range(ways)])]
    all_to_all x0 -> x1, blocking collectives: none -> 14.8 us  [on_device(): lax.all_to_all(marker_packed, 'dom', split_axis=0, concat_axis=0, tiled=T...]
    all_to_all x2 -> x0, starting transfers between devices: 14 us -> none  [the longest x1 7.12 us: on_device(): lax.all_to_all(marker_packed, 'dom', split_axis=0, concat_axis=0, tiled=T...]
    dynamic_update_slice x0 -> x15, local copies, waits for them, and re-layouts: none -> 12.6 us  [pairwise_exchange(): lax.dynamic_update_slice_in_dim(full, part, (here ^ mask) * height, axis=...]
    all_to_all x1, starting transfers between devices: 11.7 us -> 4.02 us  [on_device(): lax.all_to_all(ctf_packed, 'dom', split_axis=0, concat_axis=0, tiled=True)]
    all_gather x1, waiting for transfers between devices: 46.7 us -> 52.6 us  [on_device(): lax.all_gather(averages.astype(jnp.bfloat16), ('dom', 'cls'), axis=0, til...]
  transfers between devices with their start and end apart: 5 -> 18, of which waited for: 4 -> 15; matrix products, arithmetic and copies ran while one was open for 24% -> 12% of each run, Pallas kernels for 0% -> 0%
where the time goes in v1:
time: 400 us; the launch traced here: 399 us
  waiting for transfers between devices  188 us (47%)
  local copies, waits for them, and re-layouts  58.8 us (15%)
  matrix products  42.2 us (11%)
  blocking collectives  38.4 us (10%)
  starting transfers between devices  33.4 us (8%)
  other arithmetic  23.2 us (6%)
  between operations  15 us (4%)
    ppermute x15, waiting for transfers between devices, pairwise_exchange(): part = lax.ppermute(part, axis, [(d, d ^ mask) for d in range(ways)])  102 us
    all_gather x1, waiting for transfers between devices, on_device(): lax.all_gather(averages.astype(jnp.bfloat16), ('dom', 'cls'), axis=0, til...  52.6 us
    ppermute x15, starting transfers between devices, pairwise_exchange(): part = lax.ppermute(part, axis, [(d, d ^ mask) for d in range(ways)])  29.3 us
    unnamed x3, waiting for transfers between devices  26.4 us
    reshape x1, local copies, waits for them, and re-layouts, on_device(): every.reshape(total_classes, flat)  23.9 us
    unnamed x1, blocking collectives  23.6 us
    another operation x1, other arithmetic  18.7 us
    all_to_all x1, blocking collectives, on_device(): lax.all_to_all(marker_packed, 'dom', split_axis=0, concat_axis=0, tiled=T...  14.8 us
  transfers between devices with their start and end apart: 18, of which 15 were waited for; matrix products, arithmetic and copies ran while one was open for 12% of the time, Pallas kernels for 0%

profile of v1, /device:TPU:0, one launch (start us, length us, event | category | flops | bytes accessed | tf_op | source)
XLA Modules:
  0.0 398.7 jit_solution(1124118968322734870)
XLA Ops:
  7.2 1.6 convert_element_type.118
  9.0 0.7 and_select_fusion
  9.9 0.8 copy.19
  10.8 8.8 %fusion.24 = bf16[16,8,128,128]{3,1,2,0:T(8,128)(2,1)S(1)} fusion(bf16[32,8,128,128]{3,2,1,0:T(8,128)(2,1)} %bitcast.60, s32[128]{0:T(128)} %param.9), kind=kOutput, calls=%fused_computation.30 | convolution fusion | flops 1075871744 | bytes 12583424 | tf_op jit(solution)/shard_map/dot_general | solution.py:82
  19.6 3.2 copy.27
  23.3 18.7 %fusion.8 = (bf16[128,1,64,128]{3,2,1,0:T(8,128)(2,1)S(1)}, bf16[128,1,64,128]{3,2,1,0:T(8,128)(2,1)}) fusion(f32[128,128]{1,0:T(8,128)S(1)} %multiply_add_fusion.1, f32[64]{0:T(128)S(1)} %add_multiply_fusion, bf16[128,2,64,128]{3,2,1,0:T(8,128)(2,1)} %bitcast.59), kind=kLoop, calls=%fused_computation.17 | loop fusion | flops 12582912 | bytes 8454400 | tf_op jit(solution)/shard_map/convert
  42.0 52.6 %all-gather.2.cloned.1.call-done = bf16[512,2,64,128]{3,2,1,0:T(8,128)(2,1)} async-done(((bf16[4,2,64,128]{3,2,1,0:T(8,128)(2,1)}), bf16[512,2,64,128]{3,2,1,0:T(8,128)(2,1)}) %all-gather.2.cloned.1.call-update) | async-done | bytes 16777232 | tf_op jit(solution)/shard_map/all_gather | solution.py:98
  94.6 23.9 %copy.25 = bf16[512,2,64,128]{0,3,2,1:T(8,128)(2,1)} copy(bf16[512,2,64,128]{3,2,1,0:T(8,128)(2,1)} %all-gather.2.cloned.1.call-done) | data formatting | bytes 33554432 | tf_op jit(solution)/shard_map/reshape | solution.py:102
  118.5 13.6 %fusion = f32[128,2,64,128]{0,3,2,1:T(8,128)} fusion(bf16[512,2,64,128]{0,3,2,1:T(8,128)(2,1)} %copy.25, s32[128]{0:T(128)S(1)} %copy-done.5), kind=kOutput, calls=%fused_computation.2 | convolution fusion | flops 2147549184 | bytes 25166336 | tf_op jit(solution)/shard_map/dot_general | solution.py:101
  132.1 8.7 %copy.21 = f32[128,2,64,128]{3,2,1,0:T(8,128)} copy(f32[128,2,64,128]{0,3,2,1:T(8,128)} %fusion) | data formatting | bytes 16777216 | tf_op jit(solution)/shard_map/dot_general | solution.py:101
  140.8 9.6 %multiply_reduce_fusion = (f32[128]{0:T(128)S(1)}, bf16[128,2,64,128]{3,2,1,0:T(8,128)(2,1)S(1)}) fusion(f32[128,2,64,128]{3,2,1,0:T(8,128)} %copy.21, f32[128,64]{1,0:T(8,128)S(1)} %copy.19, s32[128,128]{1,0:T(8,128)S(1)} %add_select_fusion, bf16[128,1,64,128]{3,2,1,0:T(8,128)(2,1)} %get-tuple-element.24, bf16[128,1,64,128]{3,2,1,0:T(8,128)(2,1)S(1)} %get-tuple-element.23), kind=kOutput, calls=%fused_computation.6 | convolution fusion | flops 557842304 | bytes 16876032 | tf_op jit(solution)/shard_map/pskb,pab->pska/dot_general | solution.py:50
  150.5 3.5 convolution_convert_fusion
  153.9 0.9 broadcast_in_dim.2
  154.9 2.5 constant_dynamic-slice_fusion
  157.4 3.2 copy-done
  160.6 1.5 collective-permute-start
  162.3 14.8 %all_to_all.15 = bf16[16,1,16]{2,1,0:T(2,128)(2,1)S(1)} all-to-all(bf16[16,1,16]{2,1,0:T(2,128)(2,1)S(1)} %all_to_all.12), channel_id=1, replica_groups=mesh['dom'=16,'cls'=8] {'dom'}, dimensions={0} | all-to-all | bytes 1024 | tf_op jit(solution)/shard_map/all_to_all | solution.py:111
  177.2 0.9 collective-permute-start.1
  178.2 2.0 collective-permute-start.2
  180.2 1.5 collective-permute-start.3
  182.2 3.0 collective-permute-start.5
  185.3 0.8 constant_dynamic-update-slice_fusion.13
  186.1 7.0 %collective-permute-done.1 = bf16[1,16,16384]{2,1,0:T(8,128)(2,1)S(1)} collective-permute-done((bf16[1,16,16384]{2,1,0:T(8,128)(2,1)}, bf16[1,16,16384]{2,1,0:T(8,128)(2,1)S(1)}, u32[]{:S(2)}, u32[]{:S(2)}) %collective-permute-start.1) | collective-permute-done | bytes 524320 | tf_op jit(solution)/shard_map/ppermute | solution.py:24
  193.1 0.8 collective-permute-start.6
  193.8 0.8 constant_dynamic-update-slice_fusion.12
  194.7 9.5 %collective-permute-done.2 = bf16[1,16,16384]{2,1,0:T(8,128)(2,1)S(1)} collective-permute-done((bf16[1,16,16384]{2,1,0:T(8,128)(2,1)}, bf16[1,16,16384]{2,1,0:T(8,128)(2,1)S(1)}, u32[]{:S(2)}, u32[]{:S(2)}) %collective-permute-start.2) | collective-permute-done | bytes 524320 | tf_op jit(solution)/shard_map/ppermute | solution.py:24
  204.2 3.0 collective-permute-start.7
  207.2 0.9 constant_dynamic-update-slice_fusion.11
  208.1 0.8 constant_dynamic-update-slice_fusion.10
  208.9 3.7 collective-permute-start.9
  212.6 0.8 constant_dynamic-update-slice_fusion.9
  213.4 4.4 %collective-permute-done.5 = bf16[1,16,16384]{2,1,0:T(8,128)(2,1)S(1)} collective-permute-done((bf16[1,16,16384]{2,1,0:T(8,128)(2,1)}, bf16[1,16,16384]{2,1,0:T(8,128)(2,1)S(1)}, u32[]{:S(2)}, u32[]{:S(2)}) %collective-permute-start.5) | collective-permute-done | bytes 524320 | tf_op jit(solution)/shard_map/ppermute | solution.py:24
  217.8 5.0 %collective-permute-start.10 = (bf16[1,16,16384]{2,1,0:T(8,128)(2,1)S(1)}, bf16[1,16,16384]{2,1,0:T(8,128)(2,1)S(1)}, u32[]{:S(2)}, u32[]{:S(2)}) collective-permute-start(bf16[1,16,16384]{2,1,0:T(8,128)(2,1)S(1)} %get-tuple-element.11), channel_id=1, source_target_pairs={{0,88},{8,80},{16,72},{24,64},{32,120},{40,112},{48,104},{56,96},{... | collective-permute-start | bytes 1572872 | tf_op jit(solution)/shard_map/ppermute | solution.py:24
  222.9 0.8 constant_dynamic-update-slice_fusion.8
  223.7 6.0 %collective-permute-done.6 = bf16[1,16,16384]{2,1,0:T(8,128)(2,1)S(1)} collective-permute-done((bf16[1,16,16384]{2,1,0:T(8,128)(2,1)}, bf16[1,16,16384]{2,1,0:T(8,128)(2,1)S(1)}, u32[]{:S(2)}, u32[]{:S(2)}) %collective-permute-start.6) | collective-permute-done | bytes 524320 | tf_op jit(solution)/shard_map/ppermute | solution.py:24
  229.6 2.7 collective-permute-start.11
  232.3 0.8 constant_dynamic-update-slice_fusion.7
  233.2 9.2 %collective-permute-done.7 = bf16[1,16,16384]{2,1,0:T(8,128)(2,1)S(1)} collective-permute-done((bf16[1,16,16384]{2,1,0:T(8,128)(2,1)}, bf16[1,16,16384]{2,1,0:T(8,128)(2,1)S(1)}, u32[]{:S(2)}, u32[]{:S(2)}) %collective-permute-start.7) | collective-permute-done | bytes 524320 | tf_op jit(solution)/shard_map/ppermute | solution.py:24
  242.4 1.4 collective-permute-start.12
  243.8 0.8 constant_dynamic-update-slice_fusion.6
  244.6 9.9 %collective-permute-done.8 = bf16[1,16,16384]{2,1,0:T(8,128)(2,1)S(1)} collective-permute-done((bf16[1,16,16384]{2,1,0:T(8,128)(2,1)}, bf16[1,16,16384]{2,1,0:T(8,128)(2,1)S(1)}, u32[]{:S(2)}, u32[]{:S(2)}) %collective-permute-start.8) | collective-permute-done | bytes 524320 | tf_op jit(solution)/shard_map/ppermute | solution.py:24
  254.5 1.3 collective-permute-start.13
  255.8 0.8 constant_dynamic-update-slice_fusion.5
  256.6 10.6 %collective-permute-done.9 = bf16[1,16,16384]{2,1,0:T(8,128)(2,1)S(1)} collective-permute-done((bf16[1,16,16384]{2,1,0:T(8,128)(2,1)}, bf16[1,16,16384]{2,1,0:T(8,128)(2,1)S(1)}, u32[]{:S(2)}, u32[]{:S(2)}) %collective-permute-start.9) | collective-permute-done | bytes 524320 | tf_op jit(solution)/shard_map/ppermute | solution.py:24
  267.2 2.0 collective-permute-start.14
  269.2 0.9 constant_dynamic-update-slice_fusion.4
  270.1 5.4 %collective-permute-done.10 = bf16[1,16,16384]{2,1,0:T(8,128)(2,1)S(1)} collective-permute-done((bf16[1,16,16384]{2,1,0:T(8,128)(2,1)S(1)}, bf16[1,16,16384]{2,1,0:T(8,128)(2,1)S(1)}, u32[]{:S(2)}, u32[]{:S(2)}) %collective-permute-start.10) | collective-permute-done | bytes 524320 | tf_op jit(solution)/shard_map/ppermute | solution.py:24
  275.4 0.8 constant_dynamic-update-slice_fusion.3
  276.3 8.7 %collective-permute-done.11 = bf16[1,16,16384]{2,1,0:T(8,128)(2,1)S(1)} collective-permute-done((bf16[1,16,16384]{2,1,0:T(8,128)(2,1)S(1)}, bf16[1,16,16384]{2,1,0:T(8,128)(2,1)S(1)}, u32[]{:S(2)}, u32[]{:S(2)}) %collective-permute-start.11) | collective-permute-done | bytes 524320 | tf_op jit(solution)/shard_map/ppermute | solution.py:24
  285.0 0.8 constant_dynamic-update-slice_fusion.2
  285.8 11.2 %collective-permute-done.12 = bf16[1,16,16384]{2,1,0:T(8,128)(2,1)S(1)} collective-permute-done((bf16[1,16,16384]{2,1,0:T(8,128)(2,1)S(1)}, bf16[1,16,16384]{2,1,0:T(8,128)(2,1)S(1)}, u32[]{:S(2)}, u32[]{:S(2)}) %collective-permute-start.12) | collective-permute-done | bytes 524320 | tf_op jit(solution)/shard_map/ppermute | solution.py:24
  297.0 0.8 constant_dynamic-update-slice_fusion.1
  297.9 11.9 %collective-permute-done.13 = bf16[1,16,16384]{2,1,0:T(8,128)(2,1)S(1)} collective-permute-done((bf16[1,16,16384]{2,1,0:T(8,128)(2,1)S(1)}, bf16[1,16,16384]{2,1,0:T(8,128)(2,1)S(1)}, u32[]{:S(2)}, u32[]{:S(2)}) %collective-permute-start.13) | collective-permute-done | bytes 524320 | tf_op jit(solution)/shard_map/ppermute | solution.py:24
  309.7 0.8 constant_dynamic-update-slice_fusion
  310.6 8.5 %collective-permute-done.14 = bf16[1,16,16384]{2,1,0:T(8,128)(2,1)S(1)} collective-permute-done((bf16[1,16,16384]{2,1,0:T(8,128)(2,1)S(1)}, bf16[1,16,16384]{2,1,0:T(8,128)(2,1)S(1)}, u32[]{:S(2)}, u32[]{:S(2)}) %collective-permute-start.14) | collective-permute-done | bytes 524320 | tf_op jit(solution)/shard_map/ppermute | solution.py:24
  319.1 0.9 constant_dynamic-update-slice_fusion.14
  320.0 6.3 %fusion.41 = f32[32,16384]{1,0:T(8,128)} fusion(bf16[256,16384]{1,0:T(8,128)(2,1)} %bitcast.58, s32[256]{0:T(256)S(1)} %sub.32), kind=kOutput, calls=%fused_computation.60 | convolution fusion | flops 268443648 | bytes 10486784 | tf_op jit(solution)/shard_map/dot_general | solution.py:60
  326.6 0.7 reshape.217
  327.3 4.0 %all-to-all-start.1 = ((bf16[16,2,512]{2,1,0:T(2,128)(2,1)}), bf16[16,2,512]{2,1,0:T(2,128)(2,1)S(1)}, u32[]{:S(2)}, u32[]{:S(2)}) async-start(bf16[16,2,512]{2,1,0:T(2,128)(2,1)} %reshape.217), calls=%async_computation.1 | async-start | bytes 65536 | tf_op jit(solution)/shard_map/all_to_all | solution.py:110
  332.6 6.4 %all-to-all-done.1 = bf16[16,2,512]{2,1,0:T(2,128)(2,1)S(1)} async-done(((bf16[16,2,512]{2,1,0:T(2,128)(2,1)}), bf16[16,2,512]{2,1,0:T(2,128)(2,1)S(1)}, u32[]{:S(2)}, u32[]{:S(2)}) %all-to-all-start.1) | async-done | bytes 32800 | tf_op jit(solution)/shard_map/all_to_all | solution.py:110
  339.2 23.6 %all-reduce.1 = f32[32,64]{1,0:T(8,128)S(1)} all-reduce(f32[32,64]{1,0:T(8,128)S(1)} %fusion.40), channel_id=3, replica_groups=mesh['dom'=16,'cls'=8] {'cls'}, use_global_device_ids=true, to_apply=%region_3.4.clone | all-reduce | flops 2048 | bytes 16384
  363.3 26.4 %all-reduce.4.cloned.1.call-done = f32[32,16384]{1,0:T(8,128)} async-done(((f32[32,16384]{1,0:T(8,128)}), f32[32,16384]{1,0:T(8,128)}) %all-reduce.4.cloned.1.call-update) | async-done | bytes 2097168
  389.7 1.1 dynamic-slice_bitcast_fusion
  390.9 1.0 multiply_add_fusion
  (48 shorter events, 3.5 us)
Async XLA Ops:
  7.2 87.4 %all-gather.2.cloned.1.call-start = ((), (), s32[]{:S(2)}) async-start(), calls=%async_computation.2 | async-start | bytes 16908288 | tf_op jit(solution)/shard_map/all_gather | solution.py:98
  8.9 380.9 %all-reduce.4.cloned.1.call-start = ((), (), s32[]{:S(2)}) async-start(), calls=%async_computation.3 | async-start | bytes 4194304
  10.7 12.3 %copy-start.6 = (s32[128]{0:T(128)S(1)}, s32[128]{0:T(128)}, u32[]{:S(2)}) copy-start(s32[128]{0:T(128)} %param.11) | copy-start | bytes 1540
  10.7 12.3 %copy-start.5 = (s32[128]{0:T(128)S(1)}, s32[128]{0:T(128)}, u32[]{:S(2)}) copy-start(s32[128]{0:T(128)} %param.10) | copy-start | bytes 1540
  10.7 12.3 %copy-start.4 = (s32[128,2]{0,1:T(2,128)S(1)}, s32[128,2]{0,1:T(2,128)}, u32[]{:S(2)}) copy-start(s32[128,2]{0,1:T(2,128)} %param.12) | copy-start | bytes 3076
  157.4 3.2 copy-start
  160.6 21.6 %collective-permute-start = (bf16[1,16,16384]{2,1,0:T(8,128)(2,1)}, bf16[1,16,16384]{2,1,0:T(8,128)(2,1)S(1)}, u32[]{:S(2)}, u32[]{:S(2)}) collective-permute-start(bf16[1,16,16384]{2,1,0:T(8,128)(2,1)} %get-tuple-element.21), channel_id=1, source_target_pairs={{0,8},{8,0},{16,24},{24,16},{32,40},{40,32},{48,56},{56,48},{64,72... | collective-permute-start | bytes 1572872 | tf_op jit(solution)/shard_map/ppermute | solution.py:24
  177.2 15.8 %collective-permute-start.1 = (bf16[1,16,16384]{2,1,0:T(8,128)(2,1)}, bf16[1,16,16384]{2,1,0:T(8,128)(2,1)S(1)}, u32[]{:S(2)}, u32[]{:S(2)}) collective-permute-start(bf16[1,16,16384]{2,1,0:T(8,128)(2,1)} %get-tuple-element.20), channel_id=1, source_target_pairs={{0,16},{8,24},{16,0},{24,8},{32,48},{40,56},{48,32},{56,40},{64,80... | collective-permute-start | bytes 1572872 | tf_op jit(solution)/shard_map/ppermute | solution.py:24
  178.2 26.0 %collective-permute-start.2 = (bf16[1,16,16384]{2,1,0:T(8,128)(2,1)}, bf16[1,16,16384]{2,1,0:T(8,128)(2,1)S(1)}, u32[]{:S(2)}, u32[]{:S(2)}) collective-permute-start(bf16[1,16,16384]{2,1,0:T(8,128)(2,1)} %get-tuple-element.19), channel_id=1, source_target_pairs={{0,24},{8,16},{16,8},{24,0},{32,56},{40,48},{48,40},{56,32},{64,88... | collective-permute-start | bytes 1572872 | tf_op jit(solution)/shard_map/ppermute | solution.py:24
  180.2 27.9 %collective-permute-start.3 = (bf16[1,16,16384]{2,1,0:T(8,128)(2,1)}, bf16[1,16,16384]{2,1,0:T(8,128)(2,1)S(1)}, u32[]{:S(2)}, u32[]{:S(2)}) collective-permute-start(bf16[1,16,16384]{2,1,0:T(8,128)(2,1)} %get-tuple-element.18), channel_id=1, source_target_pairs={{0,32},{8,40},{16,48},{24,56},{32,0},{40,8},{48,16},{56,24},{64,96... | collective-permute-start | bytes 1572872 | tf_op jit(solution)/shard_map/ppermute | solution.py:24
  181.6 27.3 %collective-permute-start.4 = (bf16[1,16,16384]{2,1,0:T(8,128)(2,1)}, bf16[1,16,16384]{2,1,0:T(8,128)(2,1)S(1)}, u32[]{:S(2)}, u32[]{:S(2)}) collective-permute-start(bf16[1,16,16384]{2,1,0:T(8,128)(2,1)} %get-tuple-element.17), channel_id=1, source_target_pairs={{0,40},{8,32},{16,56},{24,48},{32,8},{40,0},{48,24},{56,16},{64,10... | collective-permute-start | bytes 1572872 | tf_op jit(solution)/shard_map/ppermute | solution.py:24
  182.2 35.6 %collective-permute-start.5 = (bf16[1,16,16384]{2,1,0:T(8,128)(2,1)}, bf16[1,16,16384]{2,1,0:T(8,128)(2,1)S(1)}, u32[]{:S(2)}, u32[]{:S(2)}) collective-permute-start(bf16[1,16,16384]{2,1,0:T(8,128)(2,1)} %get-tuple-element.16), channel_id=1, source_target_pairs={{0,48},{8,56},{16,32},{24,40},{32,16},{40,24},{48,0},{56,8},{64,11... | collective-permute-start | bytes 1572872 | tf_op jit(solution)/shard_map/ppermute | solution.py:24
  193.1 36.6 %collective-permute-start.6 = (bf16[1,16,16384]{2,1,0:T(8,128)(2,1)}, bf16[1,16,16384]{2,1,0:T(8,128)(2,1)S(1)}, u32[]{:S(2)}, u32[]{:S(2)}) collective-permute-start(bf16[1,16,16384]{2,1,0:T(8,128)(2,1)} %get-tuple-element.15), channel_id=1, source_target_pairs={{0,56},{8,48},{16,40},{24,32},{32,24},{40,16},{48,8},{56,0},{64,12... | collective-permute-start | bytes 1572872 | tf_op jit(solution)/shard_map/ppermute | solution.py:24
  204.2 38.2 %collective-permute-start.7 = (bf16[1,16,16384]{2,1,0:T(8,128)(2,1)}, bf16[1,16,16384]{2,1,0:T(8,128)(2,1)S(1)}, u32[]{:S(2)}, u32[]{:S(2)}) collective-permute-start(bf16[1,16,16384]{2,1,0:T(8,128)(2,1)} %get-tuple-element.14), channel_id=1, source_target_pairs={{0,64},{8,72},{16,80},{24,88},{32,96},{40,104},{48,112},{56,120},{... | collective-permute-start | bytes 1572872 | tf_op jit(solution)/shard_map/ppermute | solution.py:24
  208.1 46.4 %collective-permute-start.8 = (bf16[1,16,16384]{2,1,0:T(8,128)(2,1)}, bf16[1,16,16384]{2,1,0:T(8,128)(2,1)S(1)}, u32[]{:S(2)}, u32[]{:S(2)}) collective-permute-start(bf16[1,16,16384]{2,1,0:T(8,128)(2,1)} %get-tuple-element.13), channel_id=1, source_target_pairs={{0,72},{8,64},{16,88},{24,80},{32,104},{40,96},{48,120},{56,112},{... | collective-permute-start | bytes 1572872 | tf_op jit(solution)/shard_map/ppermute | solution.py:24
  208.9 58.3 %collective-permute-start.9 = (bf16[1,16,16384]{2,1,0:T(8,128)(2,1)}, bf16[1,16,16384]{2,1,0:T(8,128)(2,1)S(1)}, u32[]{:S(2)}, u32[]{:S(2)}) collective-permute-start(bf16[1,16,16384]{2,1,0:T(8,128)(2,1)} %get-tuple-element.12), channel_id=1, source_target_pairs={{0,80},{8,88},{16,64},{24,72},{32,112},{40,120},{48,96},{56,104},{... | collective-permute-start | bytes 1572872 | tf_op jit(solution)/shard_map/ppermute | solution.py:24
  217.8 57.6 %collective-permute-start.10 = (bf16[1,16,16384]{2,1,0:T(8,128)(2,1)S(1)}, bf16[1,16,16384]{2,1,0:T(8,128)(2,1)S(1)}, u32[]{:S(2)}, u32[]{:S(2)}) collective-permute-start(bf16[1,16,16384]{2,1,0:T(8,128)(2,1)S(1)} %get-tuple-element.11), channel_id=1, source_target_pairs={{0,88},{8,80},{16,72},{24,64},{32,120},{40,112},{48,104},{56,96},{... | collective-permute-start | bytes 1572872 | tf_op jit(solution)/shard_map/ppermute | solution.py:24
  229.6 55.3 %collective-permute-start.11 = (bf16[1,16,16384]{2,1,0:T(8,128)(2,1)S(1)}, bf16[1,16,16384]{2,1,0:T(8,128)(2,1)S(1)}, u32[]{:S(2)}, u32[]{:S(2)}) collective-permute-start(bf16[1,16,16384]{2,1,0:T(8,128)(2,1)S(1)} %get-tuple-element.10), channel_id=1, source_target_pairs={{0,96},{8,104},{16,112},{24,120},{32,64},{40,72},{48,80},{56,88},{... | collective-permute-start | bytes 1572872 | tf_op jit(solution)/shard_map/ppermute | solution.py:24
  242.4 54.6 %collective-permute-start.12 = (bf16[1,16,16384]{2,1,0:T(8,128)(2,1)S(1)}, bf16[1,16,16384]{2,1,0:T(8,128)(2,1)S(1)}, u32[]{:S(2)}, u32[]{:S(2)}) collective-permute-start(bf16[1,16,16384]{2,1,0:T(8,128)(2,1)S(1)} %get-tuple-element.9), channel_id=1, source_target_pairs={{0,104},{8,96},{16,120},{24,112},{32,72},{40,64},{48,88},{56,80},{... | collective-permute-start | bytes 1572872 | tf_op jit(solution)/shard_map/ppermute | solution.py:24
  254.5 55.3 %collective-permute-start.13 = (bf16[1,16,16384]{2,1,0:T(8,128)(2,1)S(1)}, bf16[1,16,16384]{2,1,0:T(8,128)(2,1)S(1)}, u32[]{:S(2)}, u32[]{:S(2)}) collective-permute-start(bf16[1,16,16384]{2,1,0:T(8,128)(2,1)S(1)} %get-tuple-element.8), channel_id=1, source_target_pairs={{0,112},{8,120},{16,96},{24,104},{32,80},{40,88},{48,64},{56,72},{... | collective-permute-start | bytes 1572872 | tf_op jit(solution)/shard_map/ppermute | solution.py:24
  267.2 51.9 %collective-permute-start.14 = (bf16[1,16,16384]{2,1,0:T(8,128)(2,1)S(1)}, bf16[1,16,16384]{2,1,0:T(8,128)(2,1)S(1)}, u32[]{:S(2)}, u32[]{:S(2)}) collective-permute-start(bf16[1,16,16384]{2,1,0:T(8,128)(2,1)S(1)} %get-tuple-element.7), channel_id=1, source_target_pairs={{0,120},{8,112},{16,104},{24,96},{32,88},{40,80},{48,72},{56,64},{... | collective-permute-start | bytes 1572872 | tf_op jit(solution)/shard_map/ppermute | solution.py:24
  276.3 50.0 %copy-start.3 = (bf16[128,64]{0,1:T(8,128)(2,1)S(1)}, bf16[128,64]{0,1:T(8,128)(2,1)}, u32[]{:S(2)}) copy-start(bf16[128,64]{0,1:T(8,128)(2,1)} %param.13) | copy-start | bytes 49156
  276.3 55.1 %copy-start.7 = (u32[128]{0:T(128)S(1)}, u32[128]{0:T(128)}, u32[]{:S(2)}) copy-start(u32[128]{0:T(128)} %constant.107) | copy-start | bytes 1540
  297.9 93.0 %copy-start.1 = (f32[4,2,64,128]{3,2,1,0:T(8,128)S(1)}, f32[4,2,64,128]{3,2,1,0:T(8,128)}, u32[]{:S(2)}) copy-start(f32[4,2,64,128]{3,2,1,0:T(8,128)} %param.14) | copy-start | bytes 786436
  297.9 93.0 %copy-start.2 = (f32[4,2,64,128]{3,2,1,0:T(8,128)S(1)}, f32[4,2,64,128]{3,2,1,0:T(8,128)}, u32[]{:S(2)}) copy-start(f32[4,2,64,128]{3,2,1,0:T(8,128)} %param.15) | copy-start | bytes 786436
  327.3 11.6 %all-to-all-start.1 = ((bf16[16,2,512]{2,1,0:T(2,128)(2,1)}), bf16[16,2,512]{2,1,0:T(2,128)(2,1)S(1)}, u32[]{:S(2)}, u32[]{:S(2)}) async-start(bf16[16,2,512]{2,1,0:T(2,128)(2,1)} %reshape.217), calls=%async_computation.1 | async-start | bytes 65536 | tf_op jit(solution)/shard_map/all_to_all | solution.py:110
Sparse Core Ops, SparseCore 0:
  11.7 82.8 all-gather.1
  326.4 63.2 all-reduce.3
